TPU v7x, 32 devices: a whole 2x2x4 slice. The times are simulated.
32 devices in a mesh: dp: 8 (over z, x), tensor: 4 (over y, core).
Axes of the slice: x: 2, y: 2, z: 4, core: 2. Of those that a mesh axis runs over, the one named last changes fastest.
Arguments:
- tokens: bfloat16 [16, 512, 768], P('dp'), may hold values from -6 to 6
- lengths: int32 [16], P('dp'), may hold values from 1 to 512, 2048 in all
- groups: int32 [16, 512], P('dp'), may hold values from 0 to 3, never falling along the last dimension, each value on 1 to 256 neighbouring positions
- key_mask: int32 [16, 512], P('dp'), may hold values 0 or 1
- w_query: bfloat16 [768, 768], P(None, 'tensor'), may hold values from -0.21875 to 0.21875
- b_query: float32 [768], P('tensor'), may hold values from -3 to 3
- w_key: bfloat16 [768, 768], P(None, 'tensor'), may hold values from -0.21875 to 0.21875
- w_value: bfloat16 [768, 768], P(None, 'tensor'), may hold values from -0.21875 to 0.21875
- b_value: float32 [768], P('tensor'), may hold values from -3 to 3
- rel_bias: float32 [12, 256], P('tensor'), may hold values from -4 to 4
- w_out: bfloat16 [768, 768], P('tensor'), may hold values from -0.625 to 0.625
- b_out: float32 [768], replicated, may hold values from -3 to 3
- gain_one: float32 [768], replicated, may hold values from 0.25 to 1.75
- shift_one: float32 [768], replicated, may hold values from -3 to 3
- w_inner: bfloat16 [768, 3072], P(None, 'tensor'), may hold values from -0.21875 to 0.21875
- b_inner: float32 [3072], P('tensor'), may hold values from -3 to 3
- w_outer: bfloat16 [3072, 768], P('tensor'), may hold values from -0.109375 to 0.109375
- b_outer: float32 [768], replicated, may hold values from -3 to 3
- gain_two: float32 [768], replicated, may hold values from 0.25 to 1.75
- shift_two: float32 [768], replicated, may hold values from -3 to 3
- cotangent: bfloat16 [16, 256, 768], P('dp'), may hold values from -24 to 24
Outputs:
- output: bfloat16 [16, 256, 768], P('dp')
- grad_tokens: bfloat16 [16, 512, 768], P('dp')
- grad_w_query: float32 [768, 768], P(None, 'tensor')
- grad_b_query: float32 [768], P('tensor')
- grad_w_key: float32 [768, 768], P(None, 'tensor')
- grad_w_value: float32 [768, 768], P(None, 'tensor')
- grad_b_value: float32 [768], P('tensor')
- grad_rel_bias: float32 [12, 256], P('tensor')
- grad_w_out: float32 [768, 768], P('tensor')
- grad_b_out: float32 [768], replicated
- grad_gain_one: float32 [768], replicated
- grad_shift_one: float32 [768], replicated
- grad_w_inner: float32 [768, 3072], P(None, 'tensor')
- grad_b_inner: float32 [3072], P('tensor')
- grad_w_outer: float32 [3072, 768], P('tensor')
- grad_b_outer: float32 [768], replicated
- grad_gain_two: float32 [768], replicated
- grad_shift_two: float32 [768], replicated
Inputs may be any that keep to these rules, and one draw needn't show every extreme that they name: `lengths`: the longest row has exactly 512 used tokens. `groups`: document ids never fall along a row; a document has at most half of 512 positions.
All inputs are finite; a program needn't handle non-finite values. No bound on the sum of `lengths` or of `key_mask` on one device may be relied on, other than what follows from the above.
Results may differ from a plain program's by a relative error of at most 0.013.
Values sent between devices are 32-bit elements; how exact they have to be, the bound alone decides.
No kernel may reach another device: no remote copies, remote signals or barrier semaphores. Data moves between devices by JAX's collectives and lax.ppermute only.
A program may use at most 128 MiB of HBM per device.

v0:
```python
import jax
import jax.numpy as jnp
from jax import lax
from jax.sharding import PartitionSpec as P


def diagonal_table(seq, width):
    span = 2 * seq
    offset = jnp.arange(span, dtype=jnp.int32)
    distance = jnp.where(offset < seq, offset, offset - span)
    bucket = jnp.clip(distance, -(width // 2), width // 2 - 1) + width // 2
    return (bucket[:, None] == jnp.arange(width, dtype=jnp.int32)[None, :]).astype(jnp.float32)


def skewed_bias(rel_bias, onehot, half, seq):
    heads = rel_bias.shape[0]
    span = 2 * seq
    line = jnp.dot(rel_bias, onehot.T, precision=lax.Precision.HIGHEST)
    tiled = jnp.tile(line, (1, half))[:, : half * (span - 2)]
    return tiled.reshape(heads, half, span - 2)[:, :, :seq]


def skewed_bias_grad(score_sum, onehot, half, seq):
    heads = score_sum.shape[0]
    span = 2 * seq
    padded = jnp.pad(score_sum, ((0, 0), (0, 0), (0, span - 2 - seq))).reshape(
        heads, half * (span - 2)
    )
    padded = jnp.pad(padded, ((0, 0), (0, 2 * half))).reshape(heads, half, span)
    along = jnp.sum(padded, axis=1)
    return jnp.dot(along, onehot, precision=lax.Precision.HIGHEST)


def allowed_keys(lengths, groups, key_mask):
    seq = groups.shape[1]
    keyed = jnp.arange(seq, dtype=jnp.int32)
    own = groups[:, 0::2]
    same = own[:, :, None] == groups[:, None, :]
    live = (keyed[None, :] < lengths[:, None]) & (key_mask == 1)
    self_key = keyed[None, :] == 2 * jnp.arange(seq // 2, dtype=jnp.int32)[:, None]
    return same & live[:, None, :] | self_key[None]


def norm_forward(value, gain, shift):
    centre = value - jnp.mean(value, axis=-1, keepdims=True)
    spread = jnp.mean(centre * centre, axis=-1, keepdims=True)
    factor = lax.rsqrt(spread + 1e-05)
    normed = centre * factor
    return (normed * gain + shift, normed, factor)


def norm_backward(grad_out, normed, factor, gain):
    grad_norm = grad_out * gain
    first_mean = jnp.mean(grad_norm, axis=-1, keepdims=True)
    second_mean = jnp.mean(grad_norm * normed, axis=-1, keepdims=True)
    grad_in = factor * (grad_norm - first_mean - normed * second_mean)
    return (grad_in, jnp.sum(grad_out * normed, axis=(0, 1)), jnp.sum(grad_out, axis=(0, 1)))


def project(left, right):
    return jnp.einsum("rld,de->rle", left, right, preferred_element_type=jnp.float32)


def project_back(left, right):
    return jnp.einsum("rle,de->rld", left, right, preferred_element_type=jnp.float32)


def weight_grad(left, right):
    return jnp.einsum("rld,rle->de", left, right, preferred_element_type=jnp.float32)


def exact_gelu(value):
    return jax.nn.gelu(value, approximate=False)


def local(
    tokens,
    lengths,
    groups,
    key_mask,
    w_query,
    b_query,
    w_key,
    w_value,
    b_value,
    rel_bias,
    w_out,
    b_out,
    gain_one,
    shift_one,
    w_inner,
    b_inner,
    w_outer,
    b_outer,
    gain_two,
    shift_two,
    cotangent,
):
    rows, seq, width = tokens.shape
    half = seq // 2
    heads, table = rel_bias.shape
    head_dim = w_query.shape[1] // heads
    wide = tokens.astype(jnp.float32)
    pooled = jnp.sum(wide.reshape(rows, half, 2, width), axis=2) * 0.5
    pooled_low = pooled.astype(jnp.bfloat16)
    query = (project(pooled_low, w_query) + b_query).astype(jnp.bfloat16)
    keys = project(tokens, w_key).astype(jnp.bfloat16)
    values = (project(tokens, w_value) + b_value).astype(jnp.bfloat16)
    query_heads = query.reshape(rows, half, heads, head_dim)
    key_heads = keys.reshape(rows, seq, heads, head_dim)
    value_heads = values.reshape(rows, seq, heads, head_dim)
    onehot = diagonal_table(seq, table)
    bias = skewed_bias(rel_bias, onehot, half, seq)
    allowed = allowed_keys(lengths, groups, key_mask)[:, None]

    def masked_scores():
        raw = (
            jnp.einsum(
                "rqhe,rkhe->rhqk", query_heads, key_heads, preferred_element_type=jnp.float32
            )
            * 0.125
            + bias[None]
        )
        return jnp.where(allowed, raw, -1e30)

    scores = masked_scores()
    top = jnp.max(scores, axis=-1, keepdims=True)
    expo = jnp.exp(scores - top)
    total = jnp.sum(expo, axis=-1, keepdims=True)
    log_total = top + jnp.log(total)
    prob_low = (expo / total).astype(jnp.bfloat16)
    context = jnp.einsum(
        "rhqk,rkhe->rqhe", prob_low, value_heads, preferred_element_type=jnp.float32
    )
    context = context.astype(jnp.bfloat16).reshape(rows, half, heads * head_dim)
    attn = lax.psum(project(context, w_out), "tensor")
    first = pooled + (attn + b_out)
    y_one, normed_one, factor_one = norm_forward(first, gain_one, shift_one)
    y_low = y_one.astype(jnp.bfloat16)
    inner = project(y_low, w_inner) + b_inner
    act = exact_gelu(inner).astype(jnp.bfloat16)
    ffn = lax.psum(project(act, w_outer), "tensor")
    second = y_one + (ffn + b_outer)
    result, normed_two, factor_two = norm_forward(second, gain_two, shift_two)
    output = result.astype(jnp.bfloat16)
    grad_out = cotangent.astype(jnp.float32)
    grad_second, grad_gain_two, grad_shift_two = norm_backward(
        grad_out, normed_two, factor_two, gain_two
    )
    grad_b_outer = jnp.sum(grad_second, axis=(0, 1))
    grad_ffn = grad_second.astype(jnp.bfloat16)
    grad_w_outer = weight_grad(act, grad_ffn)
    grad_act = project_back(grad_ffn, w_outer)
    gelu_pull = jax.vjp(exact_gelu, inner)[1]
    grad_inner = gelu_pull(grad_act)[0].astype(jnp.bfloat16)
    grad_b_inner = jnp.sum(grad_inner.astype(jnp.float32), axis=(0, 1))
    grad_w_inner = weight_grad(y_low, grad_inner)
    grad_y = grad_second + lax.psum(project_back(grad_inner, w_inner), "tensor")
    grad_first, grad_gain_one, grad_shift_one = norm_backward(
        grad_y, normed_one, factor_one, gain_one
    )
    grad_b_out = jnp.sum(grad_first, axis=(0, 1))
    grad_attn = grad_first.astype(jnp.bfloat16)
    grad_w_out = weight_grad(context, grad_attn)
    grad_context = (
        project_back(grad_attn, w_out).astype(jnp.bfloat16).reshape(rows, half, heads, head_dim)
    )
    prob = jnp.exp(masked_scores() - log_total)
    grad_prob = jnp.einsum(
        "rqhe,rkhe->rhqk", grad_context, value_heads, preferred_element_type=jnp.float32
    )
    centre_term = jnp.sum(prob * grad_prob, axis=-1, keepdims=True)
    grad_scores = (prob * (grad_prob - centre_term)).astype(jnp.bfloat16)
    score_sum = jnp.sum(grad_scores.astype(jnp.float32), axis=0)
    grad_rel_bias = skewed_bias_grad(score_sum, onehot, half, seq)
    grad_query = (
        jnp.einsum("rhqk,rkhe->rqhe", grad_scores, key_heads, preferred_element_type=jnp.float32)
        * 0.125
    ).astype(jnp.bfloat16)
    grad_keys = (
        jnp.einsum("rhqk,rqhe->rkhe", grad_scores, query_heads, preferred_element_type=jnp.float32)
        * 0.125
    ).astype(jnp.bfloat16)
    grad_values = jnp.einsum(
        "rhqk,rqhe->rkhe", prob_low, grad_context, preferred_element_type=jnp.float32
    ).astype(jnp.bfloat16)
    grad_query = grad_query.reshape(rows, half, heads * head_dim)
    grad_keys = grad_keys.reshape(rows, seq, heads * head_dim)
    grad_values = grad_values.reshape(rows, seq, heads * head_dim)
    grad_b_query = jnp.sum(grad_query.astype(jnp.float32), axis=(0, 1))
    grad_b_value = jnp.sum(grad_values.astype(jnp.float32), axis=(0, 1))
    grad_w_query = weight_grad(pooled_low, grad_query)
    grad_w_key = weight_grad(tokens, grad_keys)
    grad_w_value = weight_grad(tokens, grad_values)
    pooled_part = project_back(grad_query, w_query)
    token_part = project_back(grad_keys, w_key) + project_back(grad_values, w_value)
    pooled_sum, token_sum = lax.psum((pooled_part, token_part), "tensor")
    grad_pooled = grad_first + pooled_sum
    grad_tokens = (token_sum + jnp.repeat(grad_pooled * 0.5, 2, axis=1)).astype(jnp.bfloat16)
    (
        grad_w_query,
        grad_b_query,
        grad_w_key,
        grad_w_value,
        grad_b_value,
        grad_rel_bias,
        grad_w_out,
        grad_b_out,
        grad_gain_one,
        grad_shift_one,
        grad_w_inner,
        grad_b_inner,
        grad_w_outer,
        grad_b_outer,
        grad_gain_two,
        grad_shift_two,
    ) = lax.psum(
        (
            grad_w_query,
            grad_b_query,
            grad_w_key,
            grad_w_value,
            grad_b_value,
            grad_rel_bias,
            grad_w_out,
            grad_b_out,
            grad_gain_one,
            grad_shift_one,
            grad_w_inner,
            grad_b_inner,
            grad_w_outer,
            grad_b_outer,
            grad_gain_two,
            grad_shift_two,
        ),
        "dp",
    )
    return (
        output,
        grad_tokens,
        grad_w_query,
        grad_b_query,
        grad_w_key,
        grad_w_value,
        grad_b_value,
        grad_rel_bias,
        grad_w_out,
        grad_b_out,
        grad_gain_one,
        grad_shift_one,
        grad_w_inner,
        grad_b_inner,
        grad_w_outer,
        grad_b_outer,
        grad_gain_two,
        grad_shift_two,
    )


def solution(mesh):
    placed = (
        P("dp", None, None),
        P("dp"),
        P("dp", None),
        P("dp", None),
        P(None, "tensor"),
        P("tensor"),
        P(None, "tensor"),
        P(None, "tensor"),
        P("tensor"),
        P("tensor", None),
        P("tensor", None),
        P(),
        P(),
        P(),
        P(None, "tensor"),
        P("tensor"),
        P("tensor", None),
        P(),
        P(),
        P(),
        P("dp", None, None),
    )
    return jax.shard_map(
        local,
        mesh=mesh,
        in_specs=placed,
        out_specs=(
            P("dp", None, None),
            P("dp", None, None),
            P(None, "tensor"),
            P("tensor"),
            P(None, "tensor"),
            P(None, "tensor"),
            P("tensor"),
            P("tensor", None),
            P("tensor", None),
            P(),
            P(),
            P(),
            P(None, "tensor"),
            P("tensor"),
            P("tensor", None),
            P(),
            P(),
            P(),
        ),
        check_vma=False,
    )
```

profile of v0, /device:TPU:0, one launch (start us, length us, event | category | flops | bytes accessed | tf_op | source)
XLA Modules:
  0.0 569.3 jit_solution(7469340155090265146)
XLA Ops:
  9.1 5.0 reshape.201
  15.8 2.2 copy.45
  18.0 2.5 slice.12
  20.5 7.5 %reshape.191 = f32[3,256,1022]{2,1,0:T(8,128)} reshape(f32[3,261632]{1,0:T(4,128)} %slice.12) | data formatting | bytes 6279168 | tf_op jit(solution)/shard_map/reshape | solution.py:20
  28.8 5.6 reduce_sum.202
  44.4 45.4 %all-reduce.11.cloned.1.call-done = f32[2,256,768]{2,1,0:T(8,128)} async-done(((f32[2,256,768]{2,1,0:T(8,128)}), f32[2,256,768]{2,1,0:T(8,128)}) %all-reduce.11.cloned.1.call-update) | async-done | bytes 1572880 | tf_op jit(solution)/shard_map/psum | solution.py:136
  89.8 2.2 fusion.59
  94.0 4.5 multiply_convert_fusion.1
  99.3 1.9 fusion.18
  101.3 43.0 %all-reduce.13.cloned.1.call-done = f32[2,256,768]{2,1,0:T(8,128)} async-done(((f32[2,256,768]{2,1,0:T(8,128)}), f32[2,256,768]{2,1,0:T(8,128)}) %all-reduce.13.cloned.1.call-update) | async-done | bytes 1572880 | tf_op jit(solution)/shard_map/psum | solution.py:142
  144.3 2.0 fusion.57
  149.1 2.2 convert_reduce_fusion.2
  152.2 2.0 fusion.20
  154.9 42.4 %all-reduce.15.cloned.1.call-done = f32[2,256,768]{2,1,0:T(8,128)} async-done(((f32[2,256,768]{2,1,0:T(8,128)}), f32[2,256,768]{2,1,0:T(8,128)}) %all-reduce.15.cloned.1.call-update) | async-done | bytes 1572880 | tf_op jit(solution)/shard_map/psum | solution.py:158
  197.4 4.6 fusion.8
  206.7 2.2 convert_reduce_fusion
  211.2 1.6 fusion.40
  213.7 2.4 convolution_add_fusion
  216.8 3.7 convolution_bitcast_fusion.1
  220.6 2.5 convolution_bitcast_fusion
  229.8 3.6 pad.8
  233.4 7.6 %reshape.198 = f32[3,261632]{1,0:T(4,128)} reshape(f32[3,256,1022]{2,1,0:T(8,128)} %pad.8) | data formatting | bytes 6279168 | tf_op jit(solution)/shard_map/reshape | solution.py:26
  241.0 2.7 pad.9
  243.7 1.7 bitcast_reduce_fusion
  245.9 38.4 %all-reduce.2 = (f32[192]{0:T(256)}, f32[192]{0:T(256)}, f32[3,256]{1,0:T(4,128)}, f32[768]{0:T(1024)}, f32[768]{0:T(1024)}, /*index=5*/f32[768]{0:T(1024)}, f32...) all-reduce(f32[192]{0:T(256)S(1)} %reduce_sum.214, ...), channel_id=1, replica_groups=mesh['dp'=8,'tensor'=4] {'dp'}, use_global_device_ids=true, to_apply=%region_19.20 | all-reduce | flops 6528 | bytes 52224 | tf_op jit(solution)/shard_map/psum | solution.py:217
  284.3 26.2 %all-reduce.19.cloned.1.call-done = (f32[2,512,768]{2,1,0:T(8,128)}, f32[2,256,768]{2,1,0:T(8,128)}) async-done(((f32[2,512,768]{2,1,0:T(8,128)}, f32[2,256,768]{2,1,0:T(8,128)}), (f32[2,512,768]{2,1,0:T(8,128)}, f32[2,256,768]{2,1,0:T(8,128)})) %all-reduce.19.cloned.1.call-update) | async-done | bytes 4718608 | tf_op jit(solution)/shard_map/psum | solution.py:197
  310.5 1.6 add_multiply_fusion
  312.1 2.8 broadcast_in_dim.16
  314.9 5.3 reshape.197
  320.2 5.1 add_convert_fusion
  325.3 228.9 %all-reduce.17.cloned.1.call-done = (f32[768,192]{0,1:T(8,128)}, f32[768,192]{0,1:T(8,128)}, f32[768,192]{0,1:T(8,128)}, f32[192,768]{1,0:T(8,128)}, f32[768,768]{1,0:T(8,128)}, /*index=5*/f32[768,768]{1,0:T(8,128)}) async-done(((f32[768,192]{0,1:T(8,128)}, f32[768,192]{0,1:T(8,128)}, f32[768,192]{0,1:T(8,128)}, f32[192,768]{1,0:T(8,128)}, f32[768,768]{1,0:T(8,128)}, /*index=5*/f32[768,768]{1,0:T(8,128)}), ...) | async-done | bytes 7077904 | tf_op jit(solution)/shard_map/psum | solution.py:217
  554.2 2.0 copy.59
  (243 shorter events, 43.4 us)
Async XLA Ops:
  7.2 85.2 %copy-start = (bf16[768,768]{1,0:T(8,128)(2,1)S(1)}, bf16[768,768]{1,0:T(8,128)(2,1)}, u32[]{:S(2)}) copy-start(bf16[768,768]{1,0:T(8,128)(2,1)} %param.35) | copy-start | bytes 3538948
  7.2 82.6 %all-reduce.11.cloned.1.call-start = ((), (), s32[]{:S(2)}) async-start(), calls=%async_computation | async-start | bytes 3145728 | tf_op jit(solution)/shard_map/psum | solution.py:136
  7.3 7.5 %copy-start.78 = (s32[1024]{0:T(1024)}, s32[1024]{0:T(1024)S(1)}, u32[]{:S(2)}) copy-start(s32[1024]{0:T(1024)S(1)} %fusion.48) | copy-start | bytes 12292
  9.1 5.0 copy-start.10
  9.1 5.0 copy-start.38
  14.8 21.6 %copy-start.25 = (bf16[2,512,192]{1,2,0:T(8,128)(2,1)}, bf16[2,512,192]{1,2,0:T(8,128)(2,1)S(1)}, u32[]{:S(2)}) copy-start(bf16[2,512,192]{1,2,0:T(8,128)(2,1)S(1)} %convolution_convert_fusion.1) | copy-start | bytes 1179652
  28.8 5.7 copy-start.66
  28.8 7.1 %copy-start.29 = (bf16[768,192]{0,1:T(8,128)(2,1)S(1)}, bf16[768,192]{0,1:T(8,128)(2,1)}, u32[]{:S(2)}) copy-start(bf16[768,192]{0,1:T(8,128)(2,1)} %param.25) | copy-start | bytes 884740
  28.8 7.2 %copy-start.84 = (f32[192]{0:T(256)S(1)}, f32[192]{0:T(256)}, u32[]{:S(2)}) copy-start(f32[192]{0:T(256)} %param.26) | copy-start | bytes 2308
  42.6 47.3 %copy-start.75 = (f32[768]{0:T(1024)S(1)}, f32[768]{0:T(1024)}, u32[]{:S(2)}) copy-start(f32[768]{0:T(1024)} %param.32) | copy-start | bytes 9220
  44.1 100.2 %all-reduce.13.cloned.1.call-start = ((), (), s32[]{:S(2)}) async-start(), calls=%async_computation.1 | async-start | bytes 3145728 | tf_op jit(solution)/shard_map/psum | solution.py:142
  92.0 52.3 %copy-start.43 = (f32[2,256]{1,0:T(2,128)}, f32[2,256]{1,0:T(2,128)S(1)}, u32[]{:S(2)}) copy-start(f32[2,256]{1,0:T(2,128)S(1)} %broadcast_multiply_fusion.5) | copy-start | bytes 6148
  92.7 51.6 %copy-start.49 = (f32[2,256]{1,0:T(2,128)}, f32[2,256]{1,0:T(2,128)S(1)}, u32[]{:S(2)}) copy-start(f32[2,256]{1,0:T(2,128)S(1)} %add_rsqrt_fusion.1) | copy-start | bytes 6148
  93.9 4.5 copy-start.22
  93.9 5.4 copy-start.86
  101.2 43.1 %copy-start.81 = (f32[768]{0:T(1024)S(1)}, f32[768]{0:T(1024)}, u32[]{:S(2)}) copy-start(f32[768]{0:T(1024)} %param.38) | copy-start | bytes 9220
  101.2 96.1 %all-reduce.15.cloned.1.call-start = ((), (), s32[]{:S(2)}) async-start(), calls=%async_computation.2 | async-start | bytes 3145728 | tf_op jit(solution)/shard_map/psum | solution.py:158
  144.3 4.4 copy-start.87
  154.2 43.2 %copy-start.44 = (f32[2,256]{1,0:T(2,128)S(1)}, f32[2,256]{1,0:T(2,128)}, u32[]{:S(2)}) copy-start(f32[2,256]{1,0:T(2,128)} %copy-done.43) | copy-start | bytes 6148
  154.2 43.2 %copy-start.47 = (f32[768]{0:T(1024)S(1)}, f32[768]{0:T(1024)}, u32[]{:S(2)}) copy-start(f32[768]{0:T(1024)} %param.33) | copy-start | bytes 9220
  154.2 43.2 %copy-start.50 = (f32[2,256]{1,0:T(2,128)S(1)}, f32[2,256]{1,0:T(2,128)}, u32[]{:S(2)}) copy-start(f32[2,256]{1,0:T(2,128)} %copy-done.49) | copy-start | bytes 6148
  154.2 43.2 %copy-start.53 = (f32[2,256]{1,0:T(2,128)S(1)}, f32[2,256]{1,0:T(2,128)}, u32[]{:S(2)}) copy-start(f32[2,256]{1,0:T(2,128)} %copy-done.52) | copy-start | bytes 6148
  154.2 43.2 %copy-start.56 = (f32[2,256]{1,0:T(2,128)S(1)}, f32[2,256]{1,0:T(2,128)}, u32[]{:S(2)}) copy-start(f32[2,256]{1,0:T(2,128)} %copy-done.55) | copy-start | bytes 6148
  154.2 43.2 %copy-start.59 = (f32[768]{0:T(1024)S(1)}, f32[768]{0:T(1024)}, u32[]{:S(2)}) copy-start(f32[768]{0:T(1024)} %param.39) | copy-start | bytes 9220
  154.2 43.2 %copy-start.70 = (f32[2,256]{1,0:T(2,128)S(1)}, f32[2,256]{1,0:T(2,128)}, u32[]{:S(2)}) copy-start(f32[2,256]{1,0:T(2,128)} %copy-done.69) | copy-start | bytes 6148
  154.2 43.2 %copy-start.73 = (f32[2,256]{1,0:T(2,128)S(1)}, f32[2,256]{1,0:T(2,128)}, u32[]{:S(2)}) copy-start(f32[2,256]{1,0:T(2,128)} %copy-done.72) | copy-start | bytes 6148
  154.2 43.2 %copy-start.76 = (f32[768]{0:T(1024)S(1)}, f32[768]{0:T(1024)}, u32[]{:S(2)}) copy-start(f32[768]{0:T(1024)} %param.40) | copy-start | bytes 9220
  154.3 156.3 %all-reduce.19.cloned.1.call-start = ((), (), s32[]{:S(2)}) async-start(), calls=%async_computation.4 | async-start | bytes 9437184 | tf_op jit(solution)/shard_map/psum | solution.py:197
  216.1 4.4 copy-start.54
  216.1 4.4 copy-start.57
  216.1 4.4 copy-start.60
  216.1 338.1 %all-reduce.17.cloned.1.call-start = ((), (), s32[]{:S(2)}) async-start(), calls=%async_computation.3 | async-start | bytes 14155776 | tf_op jit(solution)/shard_map/psum | solution.py:217
  (66 other events, 121.9 us)
Sparse Core Ops, SparseCore 0:
  44.3 45.5 all-reduce.10
  101.4 42.8 all-reduce.12
  154.4 42.8 all-reduce.14
  216.2 94.2 all-reduce.18
  316.6 237.5 all-reduce.16
where the time goes:
time: 575 us; the launch traced here: 569 us
  waiting for transfers between devices  386 us (67%)
  local copies, waits for them, and re-layouts  59.8 us (10%)
  blocking collectives  38.4 us (7%)
  other arithmetic  36.3 us (6%)
  matrix products  33.2 us (6%)
  between operations  14.8 us (3%)
    psum x1, waiting for transfers between devices, local(): lax.psum((grad_w_query, grad_b_query, grad_w_key, grad_w_value, grad_b_va...  229 us
    psum x1, waiting for transfers between devices, local(): attn = lax.psum(project(context, w_out), 'tensor')  45.4 us
    psum x1, waiting for transfers between devices, local(): ffn = lax.psum(project(act, w_outer), 'tensor')  43 us
    psum x1, waiting for transfers between devices, local(): grad_y = grad_second + lax.psum(project_back(grad_inner, w_inner), 'tensor')  42.4 us
    psum x1, blocking collectives, local(): lax.psum((grad_w_query, grad_b_query, grad_w_key, grad_w_value, grad_b_va...  38.4 us
    psum x1, waiting for transfers between devices, local(): pooled_sum, token_sum = lax.psum((pooled_part, token_part), 'tensor')  26.2 us
    unnamed x192, local copies, waits for them, and re-layouts  21.6 us
  transfers between devices with their start and end apart: 5, of which 5 were waited for; matrix products, arithmetic and copies ran while one was open for 7% of the time, Pallas kernels for 0%

commit v1 on v0

--- a/solution.py
+++ b/solution.py
@@ -71,6 +71,76 @@
 
 def exact_gelu(value):
     return jax.nn.gelu(value, approximate=False)
+
+
+def swap_pairs(n, bit):
+    return [(i, i ^ bit) for i in range(n)]
+
+
+def half_of(a, which):
+    size = a.shape[0] // 2
+    return lax.dynamic_slice_in_dim(a, which * size, size, 0)
+
+
+def in_order(mine, other, which):
+    low = jnp.where(which == 0, mine, other)
+    high = jnp.where(which == 0, other, mine)
+    return jnp.concatenate([low, high], axis=0)
+
+
+def tensor_sum(part):
+    n = lax.axis_size("tensor")
+    if n != 4:
+        return lax.psum(part, "tensor")
+    core = lax.axis_index("tensor") & 1
+    got = lax.ppermute(half_of(part, 1 - core), "tensor", swap_pairs(n, 1))
+    mine = half_of(part, core) + got
+    mine = mine + lax.ppermute(mine, "tensor", swap_pairs(n, 2))
+    other = lax.ppermute(mine, "tensor", swap_pairs(n, 1))
+    return in_order(mine, other, core)
+
+
+def rows_sum(part):
+    return jnp.stack([tensor_sum(part[i]) for i in range(part.shape[0])])
+
+
+INWARD = [(0, 2), (1, 3), (6, 4), (7, 5)]
+MIDDLE = [(2, 4), (3, 5), (4, 2), (5, 3)]
+OUTWARD = [(2, 0), (3, 1), (4, 6), (5, 7)]
+
+
+def x_first(part):
+    index = lax.axis_index("dp")
+    x, z = index & 1, index >> 1
+    centre = (z == 1) | (z == 2)
+    got = lax.ppermute(half_of(part, 1 - x), "dp", swap_pairs(8, 1))
+    mine = half_of(part, x) + got
+    mine = mine + lax.ppermute(mine, "dp", INWARD)
+    mine = mine + lax.ppermute(mine, "dp", MIDDLE)
+    mine = jnp.where(centre, mine, lax.ppermute(mine, "dp", OUTWARD))
+    other = lax.ppermute(mine, "dp", swap_pairs(8, 1))
+    return in_order(mine, other, x)
+
+
+def z_first(part):
+    index = lax.axis_index("dp")
+    z = index >> 1
+    centre = (z == 1) | (z == 2)
+    own = (z == 2).astype(jnp.int32)
+    part = part + lax.ppermute(part, "dp", INWARD)
+    got = lax.ppermute(half_of(part, 1 - own), "dp", MIDDLE)
+    mine = half_of(part, own) + got
+    mine = mine + lax.ppermute(mine, "dp", [(2, 3), (3, 2), (4, 5), (5, 4)])
+    other = lax.ppermute(mine, "dp", MIDDLE)
+    full = in_order(mine, other, own)
+    return jnp.where(centre, full, lax.ppermute(full, "dp", OUTWARD))
+
+
+def dp_sum(part, cut):
+    if lax.axis_size("dp") != 8:
+        return lax.psum(part, "dp")
+    half = cut // 2
+    return jnp.concatenate([x_first(part[:half]), x_first(part[half:cut]), z_first(part[cut:])], axis=0)
 
 
 def local(
@@ -133,13 +203,13 @@
         "rhqk,rkhe->rqhe", prob_low, value_heads, preferred_element_type=jnp.float32
     )
     context = context.astype(jnp.bfloat16).reshape(rows, half, heads * head_dim)
-    attn = lax.psum(project(context, w_out), "tensor")
+    attn = rows_sum(project(context, w_out))
     first = pooled + (attn + b_out)
     y_one, normed_one, factor_one = norm_forward(first, gain_one, shift_one)
     y_low = y_one.astype(jnp.bfloat16)
     inner = project(y_low, w_inner) + b_inner
     act = exact_gelu(inner).astype(jnp.bfloat16)
-    ffn = lax.psum(project(act, w_outer), "tensor")
+    ffn = rows_sum(project(act, w_outer))
     second = y_one + (ffn + b_outer)
     result, normed_two, factor_two = norm_forward(second, gain_two, shift_two)
     output = result.astype(jnp.bfloat16)
@@ -155,7 +225,7 @@
     grad_inner = gelu_pull(grad_act)[0].astype(jnp.bfloat16)
     grad_b_inner = jnp.sum(grad_inner.astype(jnp.float32), axis=(0, 1))
     grad_w_inner = weight_grad(y_low, grad_inner)
-    grad_y = grad_second + lax.psum(project_back(grad_inner, w_inner), "tensor")
+    grad_y = grad_second + rows_sum(project_back(grad_inner, w_inner))
     grad_first, grad_gain_one, grad_shift_one = norm_backward(
         grad_y, normed_one, factor_one, gain_one
     )
@@ -194,47 +264,46 @@
     grad_w_value = weight_grad(tokens, grad_values)
     pooled_part = project_back(grad_query, w_query)
     token_part = project_back(grad_keys, w_key) + project_back(grad_values, w_value)
-    pooled_sum, token_sum = lax.psum((pooled_part, token_part), "tensor")
-    grad_pooled = grad_first + pooled_sum
-    grad_tokens = (token_sum + jnp.repeat(grad_pooled * 0.5, 2, axis=1)).astype(jnp.bfloat16)
+    token_part = token_part + jnp.repeat(pooled_part * 0.5, 2, axis=1)
+    token_sum = rows_sum(token_part)
+    grad_tokens = (token_sum + jnp.repeat(grad_first * 0.5, 2, axis=1)).astype(jnp.bfloat16)
+    small = jnp.concatenate(
+        [
+            grad_b_inner,
+            grad_b_outer,
+            grad_gain_two,
+            grad_shift_two,
+            grad_gain_one,
+            grad_shift_one,
+            grad_b_out,
+            grad_rel_bias.reshape(-1),
+            grad_b_query,
+            grad_b_value,
+        ]
+    )
+    small = jnp.pad(small, (0, 16 * width - small.shape[0])).reshape(16, width)
+    grad_w_outer = dp_sum(grad_w_outer, 576)
+    grad_w_inner = dp_sum(grad_w_inner, 576)
+    e = heads * head_dim
+    last = dp_sum(
+        jnp.concatenate([grad_w_query.T, grad_w_key.T, grad_w_value.T, grad_w_out, small], axis=0), 576
+    )
+    grad_w_query, grad_w_key, grad_w_value = (last[i * e : (i + 1) * e].T for i in range(3))
+    grad_w_out = last[3 * e : 4 * e]
+    small = last[4 * e :].reshape(-1)
     (
-        grad_w_query,
-        grad_b_query,
-        grad_w_key,
-        grad_w_value,
-        grad_b_value,
-        grad_rel_bias,
-        grad_w_out,
-        grad_b_out,
-        grad_gain_one,
-        grad_shift_one,
-        grad_w_inner,
         grad_b_inner,
-        grad_w_outer,
         grad_b_outer,
         grad_gain_two,
         grad_shift_two,
-    ) = lax.psum(
-        (
-            grad_w_query,
-            grad_b_query,
-            grad_w_key,
-            grad_w_value,
-            grad_b_value,
-            grad_rel_bias,
-            grad_w_out,
-            grad_b_out,
-            grad_gain_one,
-            grad_shift_one,
-            grad_w_inner,
-            grad_b_inner,
-            grad_w_outer,
-            grad_b_outer,
-            grad_gain_two,
-            grad_shift_two,
-        ),
-        "dp",
-    )
+        grad_gain_one,
+        grad_shift_one,
+        grad_b_out,
+        grad_rel_bias,
+    ) = (small[i * width : (i + 1) * width] for i in range(8))
+    grad_rel_bias = grad_rel_bias.reshape(heads, table)
+    grad_b_query = small[8 * width : 8 * width + e]
+    grad_b_value = small[8 * width + e : 8 * width + 2 * e]
     return (
         output,
         grad_tokens,

time: 575 us -> 472 us (0.82)
  waiting for transfers between devices: 386 us -> 191 us
  starting transfers between devices: 0.82 us -> 97.8 us
  blocking collectives: 38.4 us -> 0 us
  other arithmetic: 36.3 us -> 66 us
  local copies, waits for them, and re-layouts: 59.8 us -> 81.9 us
  between operations: 14.8 us -> 3.21 us
  matrix products: 33.2 us -> 25.4 us
    psum x5 -> x0, waiting for transfers between devices: 386 us -> none  [the longest x1 229 us: local(): lax.psum((grad_w_query, grad_b_query, grad_w_key, grad_w_value, grad_b_va...]
    ppermute x0 -> x69, waiting for transfers between devices: none -> 191 us  [the longest x6 73 us: x_first(): mine = jnp.where(centre, mine, lax.ppermute(mine, 'dp', OUTWARD))]
    ppermute x0 -> x69, starting transfers between devices: none -> 97.8 us  [the longest x3 20.7 us: z_first(): part = part + lax.ppermute(part, 'dp', INWARD)]
    psum x1 -> x0, blocking collectives: 38.4 us -> none  [local(): lax.psum((grad_w_query, grad_b_query, grad_w_key, grad_w_value, grad_b_va...]
    add x0 -> x43, other arithmetic: none -> 27.1 us  [the longest x6 6.79 us: x_first(): mine = mine + lax.ppermute(mine, 'dp', INWARD)]
    reshape x1 -> x6, local copies, waits for them, and re-layouts: 5.28 us -> 13.9 us  [the longest x1 5.34 us: local(): token_part = token_part + jnp.repeat(pooled_part * 0.5, 2, axis=1)]
    select_n x0 -> x20, other arithmetic: none -> 8.37 us  [the longest x12 7.19 us: in_order(): low = jnp.where(which == 0, mine, other)]
    dot_general x6, matrix products: 11.1 us -> 4.58 us  [weight_grad(): jnp.einsum('rld,rle->de', left, right, preferred_element_type=jnp.float32)]
  transfers between devices with their start and end apart: 5 -> 69, of which waited for: 5 -> 26; matrix products, arithmetic and copies ran while one was open for 7% -> 23% of each run, Pallas kernels for 0% -> 0%
where the time goes in v1:
time: 472 us; the launch traced here: 465 us
  waiting for transfers between devices  191 us (40%)
  starting transfers between devices  97.8 us (21%)
  local copies, waits for them, and re-layouts  81.9 us (17%)
  other arithmetic  66 us (14%)
  matrix products  25.4 us (5%)
    ppermute x6, waiting for transfers between devices, x_first(): mine = jnp.where(centre, mine, lax.ppermute(mine, 'dp', OUTWARD))  73 us
    ppermute x8, waiting for transfers between devices, tensor_sum(): mine = mine + lax.ppermute(mine, 'tensor', swap_pairs(n, 2))  34.8 us
    ppermute x6, waiting for transfers between devices, x_first(): other = lax.ppermute(mine, 'dp', swap_pairs(8, 1))  29.2 us
    ppermute x6, waiting for transfers between devices, x_first(): got = lax.ppermute(half_of(part, 1 - x), 'dp', swap_pairs(8, 1))  28.8 us
    unnamed x194, local copies, waits for them, and re-layouts  20.8 us
    ppermute x3, starting transfers between devices, z_first(): part = part + lax.ppermute(part, 'dp', INWARD)  20.7 us
    ppermute x6, waiting for transfers between devices, x_first(): mine = mine + lax.ppermute(mine, 'dp', INWARD)  19.3 us
    ppermute x6, starting transfers between devices, x_first(): mine = mine + lax.ppermute(mine, 'dp', INWARD)  18 us
  transfers between devices with their start and end apart: 69, of which 26 were waited for; matrix products, arithmetic and copies ran while one was open for 23% of the time, Pallas kernels for 0%

profile of v1, /device:TPU:0, one launch (start us, length us, event | category | flops | bytes accessed | tf_op | source)
XLA Modules:
  0.0 465.2 jit_solution(17735583598896110813)
XLA Ops:
  0.7 4.9 %reshape.246 = f32[2,256,2,768]{3,2,1,0:T(2,128)} reshape(bf16[2,512,768]{2,1,0:T(8,128)(2,1)} %param.21) | data formatting | bytes 4718592 | tf_op jit(solution)/shard_map/reshape | solution.py:174
  11.4 7.6 %reshape.231 = f32[3,256,1022]{2,1,0:T(8,128)} reshape(f32[3,261632]{1,0:T(4,128)} %slice.178) | data formatting | bytes 6279168 | tf_op jit(solution)/shard_map/reshape | solution.py:20
  22.2 5.6 %reduce_sum.202 = f32[2,256,768]{2,1,0:T(8,128)S(1)} reduce(f32[2,256,2,768]{3,2,1,0:T(2,128)} %reshape.246, f32[]{:T(128)} %constant.54.clone.1), dimensions={2}, to_apply=%region_0.0 | reduce | flops 393216 | bytes 4718596 | tf_op jit(solution)/shard_map/reduce_sum | solution.py:174
  43.8 9.8 %collective-permute-done.4 = f32[128,768]{1,0:T(8,128)S(1)} collective-permute-done((f32[128,768]{1,0:T(8,128)S(1)}, f32[128,768]{1,0:T(8,128)S(1)}, u32[]{:S(2)}, u32[]{:S(2)}) %collective-permute-start.4) | collective-permute-done | bytes 393248 | tf_op jit(solution)/shard_map/ppermute | solution.py:98
  53.7 7.8 %collective-permute-done.1 = f32[128,768]{1,0:T(8,128)S(1)} collective-permute-done((f32[128,768]{1,0:T(8,128)S(1)}, f32[128,768]{1,0:T(8,128)S(1)}, u32[]{:S(2)}, u32[]{:S(2)}) %collective-permute-start.1) | collective-permute-done | bytes 393248 | tf_op jit(solution)/shard_map/ppermute | solution.py:98
  67.1 4.5 multiply_convert_fusion.1
  77.6 9.7 %collective-permute-done.7 = f32[128,768]{1,0:T(8,128)S(1)} collective-permute-done((f32[128,768]{1,0:T(8,128)S(1)}, f32[128,768]{1,0:T(8,128)S(1)}, u32[]{:S(2)}, u32[]{:S(2)}) %collective-permute-start.7) | collective-permute-done | bytes 393248 | tf_op jit(solution)/shard_map/ppermute | solution.py:98
  87.3 7.6 %collective-permute-done.10 = f32[128,768]{1,0:T(8,128)} collective-permute-done((f32[128,768]{1,0:T(8,128)S(1)}, f32[128,768]{1,0:T(8,128)}, u32[]{:S(2)}, u32[]{:S(2)}) %collective-permute-start.10) | collective-permute-done | bytes 393248 | tf_op jit(solution)/shard_map/ppermute | solution.py:98
  108.3 3.7 collective-permute-start.64
  119.3 5.9 %collective-permute-done.59 = f32[144,768]{1,0:T(8,128)S(1)} collective-permute-done((f32[144,768]{1,0:T(8,128)S(1)}, f32[144,768]{1,0:T(8,128)S(1)}, u32[]{:S(2)}, u32[]{:S(2)}) %collective-permute-start.59) | collective-permute-done | bytes 442400 | tf_op jit(solution)/shard_map/ppermute | solution.py:116
  126.7 7.9 %collective-permute-done.54 = f32[144,768]{1,0:T(8,128)S(1)} collective-permute-done((f32[144,768]{1,0:T(8,128)S(1)}, f32[144,768]{1,0:T(8,128)S(1)}, u32[]{:S(2)}, u32[]{:S(2)}) %collective-permute-start.54) | collective-permute-done | bytes 442400 | tf_op jit(solution)/shard_map/ppermute | solution.py:116
  137.0 7.1 %collective-permute-done.44 = f32[144,768]{1,0:T(8,128)S(1)} collective-permute-done((f32[144,768]{1,0:T(8,128)S(1)}, f32[144,768]{1,0:T(8,128)S(1)}, u32[]{:S(2)}, u32[]{:S(2)}) %collective-permute-start.44) | collective-permute-done | bytes 442400 | tf_op jit(solution)/shard_map/ppermute | solution.py:116
  146.5 6.4 %collective-permute-done.39 = f32[144,768]{1,0:T(8,128)S(1)} collective-permute-done((f32[144,768]{1,0:T(8,128)S(1)}, f32[144,768]{1,0:T(8,128)S(1)}, u32[]{:S(2)}, u32[]{:S(2)}) %collective-permute-start.39) | collective-permute-done | bytes 442400 | tf_op jit(solution)/shard_map/ppermute | solution.py:116
  160.4 3.4 collective-permute-start.45
  178.8 5.3 %collective-permute-done.45 = f32[144,768]{1,0:T(8,128)} collective-permute-done((f32[144,768]{1,0:T(8,128)}, f32[144,768]{1,0:T(8,128)}, u32[]{:S(2)}, u32[]{:S(2)}) %collective-permute-start.45) | collective-permute-done | bytes 442400 | tf_op jit(solution)/shard_map/ppermute | solution.py:118
  187.4 4.9 %collective-permute-done.40 = f32[144,768]{1,0:T(8,128)} collective-permute-done((f32[144,768]{1,0:T(8,128)}, f32[144,768]{1,0:T(8,128)}, u32[]{:S(2)}, u32[]{:S(2)}) %collective-permute-start.40) | collective-permute-done | bytes 442400 | tf_op jit(solution)/shard_map/ppermute | solution.py:118
  220.0 7.6 %reshape.239 = f32[3,261632]{1,0:T(4,128)} reshape(f32[3,256,1022]{2,1,0:T(8,128)} %pad.12) | data formatting | bytes 6279168 | tf_op jit(solution)/shard_map/reshape | solution.py:26
  236.8 5.3 %reshape.237 = f32[2,512,768]{2,1,0:T(8,128)} reshape(f32[2,256,2,768]{3,2,1,0:T(2,128)} %broadcast_in_dim.22) | data formatting | bytes 6291456 | tf_op jit(solution)/shard_map/reshape | solution.py:267
  242.2 3.5 add_add_fusion
  272.2 5.3 %reshape.238 = f32[2,512,768]{2,1,0:T(8,128)} reshape(f32[2,256,2,768]{3,2,1,0:T(2,128)} %broadcast_in_dim.23) | data formatting | bytes 6291456 | tf_op jit(solution)/shard_map/reshape | solution.py:269
  278.7 15.7 %collective-permute-start.29 = (f32[208,768]{1,0:T(8,128)}, f32[208,768]{1,0:T(8,128)S(1)}, u32[]{:S(2)}, u32[]{:S(2)}) collective-permute-start(f32[208,768]{1,0:T(8,128)} %pad_maximum_fusion), channel_id=1, source_target_pairs={{0,8},{4,12},{24,16},{28,20},{1,9},{5,13},{25,17},{29,21},{2,10},{... | collective-permute-start | bytes 1916936 | tf_op jit(solution)/shard_map/ppermute | solution.py:130
  305.9 9.5 %collective-permute-done.62 = f32[144,768]{1,0:T(8,128)S(1)} collective-permute-done((f32[144,768]{1,0:T(8,128)S(1)}, f32[144,768]{1,0:T(8,128)S(1)}, u32[]{:S(2)}, u32[]{:S(2)}) %collective-permute-start.62) | collective-permute-done | bytes 442400 | tf_op jit(solution)/shard_map/ppermute | solution.py:120
  316.7 8.1 %collective-permute-done.57 = f32[144,768]{1,0:T(8,128)S(1)} collective-permute-done((f32[144,768]{1,0:T(8,128)S(1)}, f32[144,768]{1,0:T(8,128)S(1)}, u32[]{:S(2)}, u32[]{:S(2)}) %collective-permute-start.57) | collective-permute-done | bytes 442400 | tf_op jit(solution)/shard_map/ppermute | solution.py:120
  326.2 8.1 %collective-permute-done.47 = f32[144,768]{1,0:T(8,128)S(1)} collective-permute-done((f32[144,768]{1,0:T(8,128)S(1)}, f32[144,768]{1,0:T(8,128)S(1)}, u32[]{:S(2)}, u32[]{:S(2)}) %collective-permute-start.47) | collective-permute-done | bytes 442400 | tf_op jit(solution)/shard_map/ppermute | solution.py:120
  335.7 8.1 %collective-permute-done.42 = f32[144,768]{1,0:T(8,128)S(1)} collective-permute-done((f32[144,768]{1,0:T(8,128)S(1)}, f32[144,768]{1,0:T(8,128)S(1)}, u32[]{:S(2)}, u32[]{:S(2)}) %collective-permute-start.42) | collective-permute-done | bytes 442400 | tf_op jit(solution)/shard_map/ppermute | solution.py:120
  347.1 4.6 collective-permute-start.35
  352.6 6.3 %collective-permute-done.35 = f32[144,768]{1,0:T(8,128)S(1)} collective-permute-done((f32[144,768]{1,0:T(8,128)S(1)}, f32[144,768]{1,0:T(8,128)S(1)}, u32[]{:S(2)}, u32[]{:S(2)}) %collective-permute-start.35) | collective-permute-done | bytes 442400 | tf_op jit(solution)/shard_map/ppermute | solution.py:118
  361.8 19.7 %collective-permute-done.58 = f32[144,768]{1,0:T(8,128)S(1)} collective-permute-done((f32[144,768]{1,0:T(8,128)S(1)}, f32[144,768]{1,0:T(8,128)S(1)}, u32[]{:S(2)}, u32[]{:S(2)}) %collective-permute-start.58) | collective-permute-done | bytes 442400 | tf_op jit(solution)/shard_map/ppermute | solution.py:121
  382.2 4.4 collective-permute-start.25
  386.7 9.5 %collective-permute-done.43 = f32[144,768]{1,0:T(8,128)S(1)} collective-permute-done((f32[144,768]{1,0:T(8,128)S(1)}, f32[144,768]{1,0:T(8,128)S(1)}, u32[]{:S(2)}, u32[]{:S(2)}) %collective-permute-start.43) | collective-permute-done | bytes 442400 | tf_op jit(solution)/shard_map/ppermute | solution.py:121
  405.1 23.9 %collective-permute-done.37 = f32[144,768]{1,0:T(8,128)S(1)} collective-permute-done((f32[144,768]{1,0:T(8,128)S(1)}, f32[144,768]{1,0:T(8,128)S(1)}, u32[]{:S(2)}, u32[]{:S(2)}) %collective-permute-start.37) | collective-permute-done | bytes 442400 | tf_op jit(solution)/shard_map/ppermute | solution.py:120
  435.2 15.2 %collective-permute-done.27 = f32[144,768]{1,0:T(8,128)S(1)} collective-permute-done((f32[144,768]{1,0:T(8,128)S(1)}, f32[144,768]{1,0:T(8,128)S(1)}, u32[]{:S(2)}, u32[]{:S(2)}) %collective-permute-start.27) | collective-permute-done | bytes 442400 | tf_op jit(solution)/shard_map/ppermute | solution.py:120
  (489 shorter events, 205.1 us)
Async XLA Ops:
  108.3 47.0 %collective-permute-start.64 = (f32[192,768]{1,0:T(8,128)S(1)}, f32[192,768]{1,0:T(8,128)S(1)}, u32[]{:S(2)}, u32[]{:S(2)}) collective-permute-start(f32[192,768]{1,0:T(8,128)S(1)} %slice.202), channel_id=1, source_target_pairs={{0,8},{4,12},{24,16},{28,20},{1,9},{5,13},{25,17},{29,21},{2,10},{... | collective-permute-start | bytes 1769480 | tf_op jit(solution)/shard_map/ppermute | solution.py:130
  116.3 41.9 %collective-permute-start.49 = (f32[192,768]{1,0:T(8,128)S(1)}, f32[192,768]{1,0:T(8,128)S(1)}, u32[]{:S(2)}, u32[]{:S(2)}) collective-permute-start(f32[192,768]{1,0:T(8,128)S(1)} %slice.198), channel_id=1, source_target_pairs={{0,8},{4,12},{24,16},{28,20},{1,9},{5,13},{25,17},{29,21},{2,10},{... | collective-permute-start | bytes 1769480 | tf_op jit(solution)/shard_map/ppermute | solution.py:130
  117.7 26.5 %collective-permute-start.44 = (f32[144,768]{1,0:T(8,128)S(1)}, f32[144,768]{1,0:T(8,128)S(1)}, u32[]{:S(2)}, u32[]{:S(2)}) collective-permute-start(f32[144,768]{1,0:T(8,128)S(1)} %constant_dynamic-slice_fusion.4), channel_id=1, source_target_pairs={{0,4},{4,0},{8,12},{12,8},{16,20},{20,16},{24,28},{28,24},{1,5},{5... | collective-permute-start | bytes 1327112 | tf_op jit(solution)/shard_map/ppermute | solution.py:116
  125.2 27.7 %collective-permute-start.39 = (f32[144,768]{1,0:T(8,128)S(1)}, f32[144,768]{1,0:T(8,128)S(1)}, u32[]{:S(2)}, u32[]{:S(2)}) collective-permute-start(f32[144,768]{1,0:T(8,128)S(1)} %constant_dynamic-slice_fusion.5), channel_id=1, source_target_pairs={{0,4},{4,0},{8,12},{12,8},{16,20},{20,16},{24,28},{28,24},{1,5},{5... | collective-permute-start | bytes 1327112 | tf_op jit(solution)/shard_map/ppermute | solution.py:116
  134.7 25.7 %collective-permute-start.13 = (f32[128,768]{1,0:T(8,128)S(1)}, f32[128,768]{1,0:T(8,128)S(1)}, u32[]{:S(2)}, u32[]{:S(2)}) collective-permute-start(f32[128,768]{1,0:T(8,128)S(1)} %bitcast_add_fusion.3), channel_id=1, source_target_pairs={{0,2},{1,3},{2,0},{3,1},{4,6},{5,7},{6,4},{7,5},{8,10},{9,11},{10,... | collective-permute-start | bytes 1179656 | tf_op jit(solution)/shard_map/ppermute | solution.py:98
  160.4 23.7 %collective-permute-start.45 = (f32[144,768]{1,0:T(8,128)}, f32[144,768]{1,0:T(8,128)}, u32[]{:S(2)}, u32[]{:S(2)}) collective-permute-start(f32[144,768]{1,0:T(8,128)} %dynamic-slice_add_fusion.2), channel_id=1, source_target_pairs={{0,8},{4,12},{24,16},{28,20},{1,9},{5,13},{25,17},{29,21},{2,10},{... | collective-permute-start | bytes 1327112 | tf_op jit(solution)/shard_map/ppermute | solution.py:118
  163.8 28.5 %collective-permute-start.40 = (f32[144,768]{1,0:T(8,128)}, f32[144,768]{1,0:T(8,128)}, u32[]{:S(2)}, u32[]{:S(2)}) collective-permute-start(f32[144,768]{1,0:T(8,128)} %dynamic-slice_add_fusion.3), channel_id=1, source_target_pairs={{0,8},{4,12},{24,16},{28,20},{1,9},{5,13},{25,17},{29,21},{2,10},{... | collective-permute-start | bytes 1327112 | tf_op jit(solution)/shard_map/ppermute | solution.py:118
  166.6 29.1 %collective-permute-start.50 = (f32[96,768]{1,0:T(8,128)}, f32[96,768]{1,0:T(8,128)}, u32[]{:S(2)}, u32[]{:S(2)}) collective-permute-start(f32[96,768]{1,0:T(8,128)} %constant_dynamic-slice_fusion.3), channel_id=1, source_target_pairs={{8,16},{12,20},{16,8},{20,12},{9,17},{13,21},{17,9},{21,13},{10,18... | collective-permute-start | bytes 884744 | tf_op jit(solution)/shard_map/ppermute | solution.py:131
  174.6 24.2 %collective-permute-start.14 = (f32[128,768]{1,0:T(8,128)S(1)}, f32[128,768]{1,0:T(8,128)S(1)}, u32[]{:S(2)}, u32[]{:S(2)}) collective-permute-start(f32[128,768]{1,0:T(8,128)S(1)} %add.346), channel_id=1, source_target_pairs={{0,1},{1,0},{2,3},{3,2},{4,5},{5,4},{6,7},{7,6},{8,9},{9,8},{10,11... | collective-permute-start | bytes 1179656 | tf_op jit(solution)/shard_map/ppermute | solution.py:99
  176.6 23.9 %collective-permute-start.17 = (f32[128,768]{1,0:T(8,128)S(1)}, f32[128,768]{1,0:T(8,128)S(1)}, u32[]{:S(2)}, u32[]{:S(2)}) collective-permute-start(f32[128,768]{1,0:T(8,128)S(1)} %add.348), channel_id=1, source_target_pairs={{0,1},{1,0},{2,3},{3,2},{4,5},{5,4},{6,7},{7,6},{8,9},{9,8},{10,11... | collective-permute-start | bytes 1179656 | tf_op jit(solution)/shard_map/ppermute | solution.py:99
  184.1 72.7 %collective-permute-start.66 = (f32[96,768]{1,0:T(8,128)}, f32[96,768]{1,0:T(8,128)}, u32[]{:S(2)}, u32[]{:S(2)}) collective-permute-start(f32[96,768]{1,0:T(8,128)} %dynamic-slice_add_fusion.5), channel_id=1, source_target_pairs={{8,12},{12,8},{16,20},{20,16},{9,13},{13,9},{17,21},{21,17},{10,14... | collective-permute-start | bytes 884744 | tf_op jit(solution)/shard_map/ppermute | solution.py:133
  192.3 75.0 %collective-permute-start.61 = (f32[144,768]{1,0:T(8,128)}, f32[144,768]{1,0:T(8,128)}, u32[]{:S(2)}, u32[]{:S(2)}) collective-permute-start(f32[144,768]{1,0:T(8,128)} %add.385), channel_id=1, source_target_pairs={{8,16},{12,20},{16,8},{20,12},{9,17},{13,21},{17,9},{21,13},{10,18... | collective-permute-start | bytes 1327112 | tf_op jit(solution)/shard_map/ppermute | solution.py:119
  195.7 83.0 %collective-permute-start.56 = (f32[144,768]{1,0:T(8,128)}, f32[144,768]{1,0:T(8,128)}, u32[]{:S(2)}, u32[]{:S(2)}) collective-permute-start(f32[144,768]{1,0:T(8,128)} %add.382), channel_id=1, source_target_pairs={{8,16},{12,20},{16,8},{20,12},{9,17},{13,21},{17,9},{21,13},{10,18... | collective-permute-start | bytes 1327112 | tf_op jit(solution)/shard_map/ppermute | solution.py:119
  198.8 64.0 %collective-permute-start.51 = (f32[96,768]{1,0:T(8,128)}, f32[96,768]{1,0:T(8,128)}, u32[]{:S(2)}, u32[]{:S(2)}) collective-permute-start(f32[96,768]{1,0:T(8,128)} %dynamic-slice_add_fusion.6), channel_id=1, source_target_pairs={{8,12},{12,8},{16,20},{20,16},{9,13},{13,9},{17,21},{21,17},{10,14... | collective-permute-start | bytes 884744 | tf_op jit(solution)/shard_map/ppermute | solution.py:133
  200.4 95.2 %collective-permute-start.46 = (f32[144,768]{1,0:T(8,128)}, f32[144,768]{1,0:T(8,128)}, u32[]{:S(2)}, u32[]{:S(2)}) collective-permute-start(f32[144,768]{1,0:T(8,128)} %add.375), channel_id=1, source_target_pairs={{8,16},{12,20},{16,8},{20,12},{9,17},{13,21},{17,9},{21,13},{10,18... | collective-permute-start | bytes 1327112 | tf_op jit(solution)/shard_map/ppermute | solution.py:119
  256.7 40.7 %collective-permute-start.41 = (f32[144,768]{1,0:T(8,128)}, f32[144,768]{1,0:T(8,128)}, u32[]{:S(2)}, u32[]{:S(2)}) collective-permute-start(f32[144,768]{1,0:T(8,128)} %add.372), channel_id=1, source_target_pairs={{8,16},{12,20},{16,8},{20,12},{9,17},{13,21},{17,9},{21,13},{10,18... | collective-permute-start | bytes 1327112 | tf_op jit(solution)/shard_map/ppermute | solution.py:119
  262.8 35.8 %collective-permute-start.67 = (f32[96,768]{1,0:T(8,128)}, f32[96,768]{1,0:T(8,128)}, u32[]{:S(2)}, u32[]{:S(2)}) collective-permute-start(f32[96,768]{1,0:T(8,128)} %add.389), channel_id=1, source_target_pairs={{8,16},{12,20},{16,8},{20,12},{9,17},{13,21},{17,9},{21,13},{10,18... | collective-permute-start | bytes 884744 | tf_op jit(solution)/shard_map/ppermute | solution.py:134
  267.2 33.1 %collective-permute-start.52 = (f32[96,768]{1,0:T(8,128)}, f32[96,768]{1,0:T(8,128)}, u32[]{:S(2)}, u32[]{:S(2)}) collective-permute-start(f32[96,768]{1,0:T(8,128)} %add.380), channel_id=1, source_target_pairs={{8,16},{12,20},{16,8},{20,12},{9,17},{13,21},{17,9},{21,13},{10,18... | collective-permute-start | bytes 884744 | tf_op jit(solution)/shard_map/ppermute | solution.py:134
  278.7 66.7 %collective-permute-start.29 = (f32[208,768]{1,0:T(8,128)}, f32[208,768]{1,0:T(8,128)S(1)}, u32[]{:S(2)}, u32[]{:S(2)}) collective-permute-start(f32[208,768]{1,0:T(8,128)} %pad_maximum_fusion), channel_id=1, source_target_pairs={{0,8},{4,12},{24,16},{28,20},{1,9},{5,13},{25,17},{29,21},{2,10},{... | collective-permute-start | bytes 1916936 | tf_op jit(solution)/shard_map/ppermute | solution.py:130
  297.5 49.6 %collective-permute-start.18 = (f32[256,768]{1,0:T(8,128)S(1)}, f32[256,768]{1,0:T(8,128)S(1)}, u32[]{:S(2)}, u32[]{:S(2)}) collective-permute-start(f32[256,768]{1,0:T(8,128)S(1)} %copy-done.43), channel_id=1, source_target_pairs={{0,1},{1,0},{2,3},{3,2},{4,5},{5,4},{6,7},{7,6},{8,9},{9,8},{10,11... | collective-permute-start | bytes 2359304 | tf_op jit(solution)/shard_map/ppermute | solution.py:96
  298.6 53.2 %collective-permute-start.21 = (f32[256,768]{1,0:T(8,128)S(1)}, f32[256,768]{1,0:T(8,128)S(1)}, u32[]{:S(2)}, u32[]{:S(2)}) collective-permute-start(f32[256,768]{1,0:T(8,128)S(1)} %copy-done.44), channel_id=1, source_target_pairs={{0,1},{1,0},{2,3},{3,2},{4,5},{5,4},{6,7},{7,6},{8,9},{9,8},{10,11... | collective-permute-start | bytes 2359304 | tf_op jit(solution)/shard_map/ppermute | solution.py:96
  334.3 66.7 %collective-permute-start.68 = (f32[192,768]{1,0:T(8,128)S(1)}, f32[192,768]{1,0:T(8,128)S(1)}, u32[]{:S(2)}, u32[]{:S(2)}) collective-permute-start(f32[192,768]{1,0:T(8,128)S(1)} %pad_maximum_fusion.6), channel_id=1, source_target_pairs={{8,0},{12,4},{16,24},{20,28},{9,1},{13,5},{17,25},{21,29},{10,2},{... | collective-permute-start | bytes 1769480 | tf_op jit(solution)/shard_map/ppermute | solution.py:136
  343.8 86.6 %collective-permute-start.53 = (f32[192,768]{1,0:T(8,128)S(1)}, f32[192,768]{1,0:T(8,128)S(1)}, u32[]{:S(2)}, u32[]{:S(2)}) collective-permute-start(f32[192,768]{1,0:T(8,128)S(1)} %pad_maximum_fusion.5), channel_id=1, source_target_pairs={{8,0},{12,4},{16,24},{20,28},{9,1},{13,5},{17,25},{21,29},{10,2},{... | collective-permute-start | bytes 1769480 | tf_op jit(solution)/shard_map/ppermute | solution.py:136
  358.9 23.2 %collective-permute-start.63 = (f32[144,768]{1,0:T(8,128)S(1)}, f32[144,768]{1,0:T(8,128)S(1)}, u32[]{:S(2)}, u32[]{:S(2)}) collective-permute-start(f32[144,768]{1,0:T(8,128)S(1)} %broadcast_select_fusion.5), channel_id=1, source_target_pairs={{0,4},{4,0},{8,12},{12,8},{16,20},{20,16},{24,28},{28,24},{1,5},{5... | collective-permute-start | bytes 1327112 | tf_op jit(solution)/shard_map/ppermute | solution.py:121
  359.5 22.0 %collective-permute-start.58 = (f32[144,768]{1,0:T(8,128)S(1)}, f32[144,768]{1,0:T(8,128)S(1)}, u32[]{:S(2)}, u32[]{:S(2)}) collective-permute-start(f32[144,768]{1,0:T(8,128)S(1)} %broadcast_select_fusion.6), channel_id=1, source_target_pairs={{0,4},{4,0},{8,12},{12,8},{16,20},{20,16},{24,28},{28,24},{1,5},{5... | collective-permute-start | bytes 1327112 | tf_op jit(solution)/shard_map/ppermute | solution.py:121
  361.2 35.8 %collective-permute-start.48 = (f32[144,768]{1,0:T(8,128)S(1)}, f32[144,768]{1,0:T(8,128)S(1)}, u32[]{:S(2)}, u32[]{:S(2)}) collective-permute-start(f32[144,768]{1,0:T(8,128)S(1)} %broadcast_select_fusion.7), channel_id=1, source_target_pairs={{0,4},{4,0},{8,12},{12,8},{16,20},{20,16},{24,28},{28,24},{1,5},{5... | collective-permute-start | bytes 1327112 | tf_op jit(solution)/shard_map/ppermute | solution.py:121
  398.6 35.3 %collective-permute-start.19 = (f32[256,768]{1,0:T(8,128)S(1)}, f32[256,768]{1,0:T(8,128)S(1)}, u32[]{:S(2)}, u32[]{:S(2)}) collective-permute-start(f32[256,768]{1,0:T(8,128)S(1)} %bitcast_add_fusion.1), channel_id=1, source_target_pairs={{0,2},{1,3},{2,0},{3,1},{4,6},{5,7},{6,4},{7,5},{8,10},{9,11},{10,... | collective-permute-start | bytes 2359304 | tf_op jit(solution)/shard_map/ppermute | solution.py:98
  401.0 28.1 %collective-permute-start.37 = (f32[144,768]{1,0:T(8,128)S(1)}, f32[144,768]{1,0:T(8,128)S(1)}, u32[]{:S(2)}, u32[]{:S(2)}) collective-permute-start(f32[144,768]{1,0:T(8,128)S(1)} %add.370), channel_id=1, source_target_pairs={{8,0},{12,4},{16,24},{20,28},{9,1},{13,5},{17,25},{21,29},{10,2},{... | collective-permute-start | bytes 1327112 | tf_op jit(solution)/shard_map/ppermute | solution.py:120
  402.4 31.6 %collective-permute-start.22 = (f32[256,768]{1,0:T(8,128)S(1)}, f32[256,768]{1,0:T(8,128)S(1)}, u32[]{:S(2)}, u32[]{:S(2)}) collective-permute-start(f32[256,768]{1,0:T(8,128)S(1)} %bitcast_add_fusion), channel_id=1, source_target_pairs={{0,2},{1,3},{2,0},{3,1},{4,6},{5,7},{6,4},{7,5},{8,10},{9,11},{10,... | collective-permute-start | bytes 2359304 | tf_op jit(solution)/shard_map/ppermute | solution.py:98
  403.8 49.2 %collective-permute-start.33 = (f32[208,768]{1,0:T(8,128)S(1)}, f32[208,768]{1,0:T(8,128)S(1)}, u32[]{:S(2)}, u32[]{:S(2)}) collective-permute-start(f32[208,768]{1,0:T(8,128)S(1)} %pad_maximum_fusion.1), channel_id=1, source_target_pairs={{8,0},{12,4},{16,24},{20,28},{9,1},{13,5},{17,25},{21,29},{10,2},{... | collective-permute-start | bytes 1916936 | tf_op jit(solution)/shard_map/ppermute | solution.py:136
  433.9 21.9 %collective-permute-start.20 = (f32[256,768]{1,0:T(8,128)S(1)}, f32[256,768]{1,0:T(8,128)}, u32[]{:S(2)}, u32[]{:S(2)}) collective-permute-start(f32[256,768]{1,0:T(8,128)S(1)} %add.355), channel_id=1, source_target_pairs={{0,1},{1,0},{2,3},{3,2},{4,5},{5,4},{6,7},{7,6},{8,9},{9,8},{10,11... | collective-permute-start | bytes 2359304 | tf_op jit(solution)/shard_map/ppermute | solution.py:99
  435.2 21.9 %collective-permute-start.23 = (f32[256,768]{1,0:T(8,128)S(1)}, f32[256,768]{1,0:T(8,128)}, u32[]{:S(2)}, u32[]{:S(2)}) collective-permute-start(f32[256,768]{1,0:T(8,128)S(1)} %add.357), channel_id=1, source_target_pairs={{0,1},{1,0},{2,3},{3,2},{4,5},{5,4},{6,7},{7,6},{8,9},{9,8},{10,11... | collective-permute-start | bytes 2359304 | tf_op jit(solution)/shard_map/ppermute | solution.py:99
  (134 other events, 851.6 us)
